TPU v7x, 32 devices: a whole 2x2x4 slice. The times are simulated.
32 devices in a mesh: vol: 1, slab: 8 (over z, x), filt: 4 (over y, core).
Axes of the slice: x: 2, y: 2, z: 4, core: 2. Of those that a mesh axis runs over, the one named last changes fastest.
Arguments:
- volume: bfloat16 [32, 64, 64, 256], P(('vol', 'slab', 'filt')), may hold values from -6 to 6
- weights: bfloat16 [256, 27, 256], P('filt'), may hold values from -0.078125 to 0.078125
- bias: bfloat16 [256], P('filt'), may hold values from -3 to 3
Outputs:
- activated: bfloat16 [32, 64, 64, 256], P(('vol', 'slab'), None, None, 'filt')
All inputs are finite; a program needn't handle non-finite values.
Results may differ from a plain program's by a relative error of at most 0.001.
Values may be sent and summed in bfloat16 or wider, within the bound.
A program may use at most 448 MiB of HBM per device.

v0:
```python
import jax
import jax.numpy as jnp
from jax import lax
from jax.sharding import PartitionSpec as P


def extended(cells, sides, width):
    for axis, dim in sides:
        count = lax.axis_size(axis)
        ends = count - 1
        head = lax.slice_in_dim(cells, 0, width, axis=dim)
        tail = lax.slice_in_dim(cells, cells.shape[dim] - width, cells.shape[dim], axis=dim)
        cells = jnp.concatenate(
            [
                lax.ppermute(tail, axis, [(i, (i + 1) % count) for i in range(ends)]),
                cells,
                lax.ppermute(head, axis, [((i + 1) % count, i) for i in range(ends)]),
            ],
            axis=dim,
        )
    return cells


def convolve(padded, weights, bias):
    planes = padded.shape[0] - 2
    rows = padded.shape[1]
    cols = padded.shape[2]
    chans = padded.shape[3]
    outs = weights.shape[0]
    framed = jnp.pad(padded, ((0, 0), (1, 1), (1, 1), (0, 0)))
    total = jnp.zeros((planes, rows * cols, outs), jnp.float32)
    for tap_z in range(3):
        for tap_y in range(3):
            for tap_x in range(3):
                window = framed[
                    tap_z : tap_z + planes, tap_y : tap_y + rows, tap_x : tap_x + cols
                ].reshape(planes, rows * cols, chans)
                tap_weight = weights[:, 9 * tap_z + 3 * tap_y + tap_x, :]
                total = total + jnp.einsum(
                    "zpi,oi->zpo", window, tap_weight, preferred_element_type=jnp.float32
                )
    shifted = total + bias.astype(jnp.float32)[None, None, :]
    result = jnp.where(shifted > 0, shifted, 0.3 * shifted)
    return result.astype(jnp.bfloat16).reshape(planes, rows, cols, outs)


def body(volume, weights, bias):
    slab_planes = lax.all_gather(volume, "filt", axis=0, tiled=True)
    padded = extended(slab_planes, (("slab", 0),), 1)
    return convolve(padded, weights, bias)


def solution(mesh):
    return jax.shard_map(
        body,
        mesh=mesh,
        in_specs=(P(("vol", "slab", "filt"), None, None, None), P("filt", None, None), P("filt")),
        out_specs=P(("vol", "slab"), None, None, "filt"),
        check_vma=False,
    )
```

profile of v0, /device:TPU:0, one launch (start us, length us, event | category | flops | bytes accessed | tf_op | source)
XLA Modules:
  0.0 524.3 jit_solution(2084521685995472989)
XLA Ops:
  7.3 62.7 %all-gather.2.cloned.1.call-done = bf16[4,64,64,256]{3,2,1,0:T(8,128)(2,1)} async-done(((bf16[1,64,64,256]{3,2,1,0:T(8,128)(2,1)}), bf16[4,64,64,256]{3,2,1,0:T(8,128)(2,1)}) %all-gather.2.cloned.1.call-update) | async-done | bytes 8388624 | tf_op jit(solution)/shard_map/all_gather | solution.py:48
  78.4 4.6 fusion.57
  82.9 83.6 %collective-permute-done = bf16[1,64,64,256]{3,2,1,0:T(8,128)(2,1)S(1)} collective-permute-done((bf16[1,64,64,256]{3,2,1,0:T(8,128)(2,1)S(1)}, bf16[1,64,64,256]{3,2,1,0:T(8,128)(2,1)S(1)}, u32[]{:S(2)}, u32[]{:S(2)}) %collective-permute-start) | collective-permute-done | bytes 2097184 | tf_op jit(solution)/shard_map/ppermute | solution.py:15
  169.3 21.5 %select_maximum_fusion = bf16[6,66,66,256]{3,2,1,0:T(8,128)(2,1)} fusion(bf16[1,64,64,256]{3,2,1,0:T(8,128)(2,1)S(1)} %collective-permute-done.1, bf16[4,64,64,256]{3,2,1,0:T(8,128)(2,1)S(1)} %copy-done, bf16[1,64,64,256]{3,2,1,0:T(8,128)(2,1)S(1)} %collective-permute-done), kind=kLoop, calls=%fused_computation.7 | loop fusion | flops 127125504 | bytes 25964544 | tf_op jit(solution)/shard_map/concatenate | solution.py:13
  190.8 126.1 %fusion.111 = (bf16[4,64,64,256]{3,2,1,0:T(8,128)(2,1)}, bf16[4,64,64,256]{3,2,1,0:T(8,128)(2,1)}, bf16[4,64,64,256]{3,2,1,0:T(8,128)(2,1)}, bf16[4,64,64,256]{3...) fusion(bf16[6,66,66,256]{3,2,1,0:T(8,128)(2,1)} %select_maximum, ...), kind=kLoop, calls=%fused_computation.122 | loop fusion | bytes 318767104 | tf_op jit(solution)/shard_map/slice | solution.py:35
  316.9 32.3 %fusion.112 = (bf16[4,64,64,256]{3,2,1,0:T(8,128)(2,1)}, bf16[4,64,64,256]{3,2,1,0:T(8,128)(2,1)}, bf16[4,64,64,256]{3,2,1,0:T(8,128)(2,1)}, bf16[4,64,64,256]{3,2,1,0:T(8,128)(2,1)}, bf16[4,64,64,256]{3,2,1,0:T(8,128)(2,1)}) fusion(bf16[6,66,66,256]{3,2,1,0:T(8,128)(2,1)} %select_maximum_fusion), kind=kLoop, calls=%fused_computation.123 | loop fusion | bytes 83886080 | tf_op jit(solution)/shard_map/slice | solution.py:35
  349.2 8.2 %fusion.59 = f32[4,4096,64]{1,2,0:T(8,128)} fusion(bf16[4,4096,256]{2,1,0:T(8,128)(2,1)} %bitcast.221, bf16[64,27,256]{2,0,1:T(8,128)(2,1)S(1)} %copy-done.6), kind=kOutput, calls=%fused_computation.70 | convolution fusion | flops 536870912 | bytes 12615680 | tf_op jit(solution)/shard_map/zpi,oi->zpo/dot_general | solution.py:39
  357.4 4.6 fusion.61
  362.1 4.7 fusion.63
  366.8 4.6 fusion.65
  371.5 4.7 fusion.67
  376.1 4.6 fusion.69
  380.7 4.7 fusion.71
  385.4 4.6 fusion.73
  390.0 4.7 fusion.77
  394.8 4.6 fusion.79
  399.4 4.8 fusion.81
  408.6 4.6 fusion.75
  413.2 4.6 fusion.34
  417.8 4.6 fusion.36
  422.4 4.6 fusion.38
  431.6 4.6 fusion.44
  436.2 4.6 fusion.46
  440.8 4.6 fusion.48
  445.4 4.7 fusion.50
  450.2 4.6 fusion.52
  454.8 4.6 fusion.54
  459.3 4.7 fusion.32
  464.0 4.6 fusion.40
  468.6 24.2 %fusion.29 = f32[4,4096,64]{1,2,0:T(8,128)} fusion(f32[4,4096,64]{1,2,0:T(8,128)} %fusion.57, f32[4,4096,64]{1,2,0:T(8,128)} %fusion.59, f32[4,4096,64]{1,2,0:T(8,128)} %fusion.61, f32[4,4096,64]{1,2,0:T(8,128)} %fusion.63, f32[4,4096,64]{1,2,0:T(8,128)} %fusion.65, f32[4,4096,64]{1,2,0:T(8,128)} %fusion.67, f32[4,4096,64]{1,2,0:T(8,128)} %fusion.69, ...), kind=kOutput, calls=%fused_computation.40 | convolution fusion | flops 550502400 | bytes 67141632 | tf_op jit(solution)/shard_map/zpi,oi->zpo/dot_general | solution.py:39
  492.8 19.7 %fusion.31 = bf16[4,4096,64]{1,2,0:T(8,128)(2,1)} fusion(f32[4,4096,64]{1,2,0:T(8,128)} %fusion.32, f32[4,4096,64]{1,2,0:T(8,128)} %fusion.34, f32[4,4096,64]{1,2,0:T(8,128)} %fusion.36, f32[4,4096,64]{1,2,0:T(8,128)} %fusion.38, f32[4,4096,64]{1,2,0:T(8,128)} %fusion.40, f32[4,4096,64]{1,2,0:T(8,128)} %fusion.42, f32[4,4096,64]{1,2,0:T(8,128)} %fusion.44, ...), kind=kOutput, calls=%fused_computation.42 | convolution fusion | flops 555745280 | bytes 65044992 | tf_op jit(solution)/shard_map/zpi,oi->zpo/dot_general | solution.py:39
  512.5 4.8 copy.6
  (142 shorter events, 21.0 us)
Async XLA Ops:
  6.5 71.2 %copy-start.8 = (bf16[64]{0:T(256)(128)(2,1)S(1)}, bf16[64]{0:T(256)(128)(2,1)}, u32[]{:S(2)}) copy-start(bf16[64]{0:T(256)(128)(2,1)} %param.5) | copy-start | bytes 388
  6.5 71.8 %copy-start.6 = (bf16[64,27,256]{2,0,1:T(8,128)(2,1)S(1)}, bf16[64,27,256]{2,0,1:T(8,128)(2,1)}, u32[]{:S(2)}) copy-start(bf16[64,27,256]{2,0,1:T(8,128)(2,1)} %param.4) | copy-start | bytes 2654212
  6.5 63.4 %all-gather.2.cloned.1.call-start = ((), (), s32[]{:S(2)}) async-start(), calls=%async_computation | async-start | bytes 10485760 | tf_op jit(solution)/shard_map/all_gather | solution.py:48
  69.9 8.4 %copy-start = (bf16[4,64,64,256]{3,2,1,0:T(8,128)(2,1)S(1)}, bf16[4,64,64,256]{3,2,1,0:T(8,128)(2,1)}, u32[]{:S(2)}) copy-start(bf16[4,64,64,256]{3,2,1,0:T(8,128)(2,1)} %all-gather.2.cloned.1.call-done) | copy-start | bytes 25165828
  72.8 93.7 %collective-permute-start = (bf16[1,64,64,256]{3,2,1,0:T(8,128)(2,1)S(1)}, bf16[1,64,64,256]{3,2,1,0:T(8,128)(2,1)S(1)}, u32[]{:S(2)}, u32[]{:S(2)}) collective-permute-start(bf16[1,64,64,256]{3,2,1,0:T(8,128)(2,1)S(1)} %get-tuple-element.31), channel_id=1, source_target_pairs={{0,4},{4,8},{8,12},{12,16},{16,20},{20,24},{24,28},{1,5},{5,9},{9,... | collective-permute-start | bytes 6291464 | tf_op jit(solution)/shard_map/ppermute | solution.py:15
  76.5 90.1 %collective-permute-start.1 = (bf16[1,64,64,256]{3,2,1,0:T(8,128)(2,1)S(1)}, bf16[1,64,64,256]{3,2,1,0:T(8,128)(2,1)S(1)}, u32[]{:S(2)}, u32[]{:S(2)}) collective-permute-start(bf16[1,64,64,256]{3,2,1,0:T(8,128)(2,1)S(1)} %get-tuple-element.32), channel_id=1, source_target_pairs={{4,0},{8,4},{12,8},{16,12},{20,16},{24,20},{28,24},{5,1},{9,5},{13... | collective-permute-start | bytes 6291464 | tf_op jit(solution)/shard_map/ppermute | solution.py:17
  349.2 12.8 %slice-start.34 = ((s8[8388608]{0:T(1024)(128)(4,1)}), s8[4194304]{0:T(1024)(128)(4,1)S(1)}, s32[]{:S(2)}) async-start(s8[8388608]{0:T(1024)(128)(4,1)} %bitcast.214), calls=%async_computation.35 | async-start | bytes 8388608
  357.4 9.4 %slice-start.32 = ((s8[8388608]{0:T(1024)(128)(4,1)}), s8[4194304]{0:T(1024)(128)(4,1)S(1)}, s32[]{:S(2)}) async-start(s8[8388608]{0:T(1024)(128)(4,1)} %bitcast.211), calls=%async_computation.33 | async-start | bytes 8388608
  362.1 9.4 %slice-start.30 = ((s8[8388608]{0:T(1024)(128)(4,1)}), s8[4194304]{0:T(1024)(128)(4,1)S(1)}, s32[]{:S(2)}) async-start(s8[8388608]{0:T(1024)(128)(4,1)} %bitcast.208), calls=%async_computation.31 | async-start | bytes 8388608
  366.8 9.3 %slice-start.28 = ((s8[8388608]{0:T(1024)(128)(4,1)}), s8[4194304]{0:T(1024)(128)(4,1)S(1)}, s32[]{:S(2)}) async-start(s8[8388608]{0:T(1024)(128)(4,1)} %bitcast.205), calls=%async_computation.29 | async-start | bytes 8388608
  371.5 9.3 %slice-start.26 = ((s8[8388608]{0:T(1024)(128)(4,1)}), s8[4194304]{0:T(1024)(128)(4,1)S(1)}, s32[]{:S(2)}) async-start(s8[8388608]{0:T(1024)(128)(4,1)} %bitcast.202), calls=%async_computation.27 | async-start | bytes 8388608
  376.1 9.3 %slice-start.24 = ((s8[8388608]{0:T(1024)(128)(4,1)}), s8[4194304]{0:T(1024)(128)(4,1)S(1)}, s32[]{:S(2)}) async-start(s8[8388608]{0:T(1024)(128)(4,1)} %bitcast.199), calls=%async_computation.25 | async-start | bytes 8388608
  380.7 9.3 %slice-start.42 = ((s8[8388608]{0:T(1024)(128)(4,1)}), s8[4194304]{0:T(1024)(128)(4,1)S(1)}, s32[]{:S(2)}) async-start(s8[8388608]{0:T(1024)(128)(4,1)} %bitcast.228), calls=%async_computation.43 | async-start | bytes 8388608
  385.4 9.4 %slice-start.40 = ((s8[8388608]{0:T(1024)(128)(4,1)}), s8[4194304]{0:T(1024)(128)(4,1)S(1)}, s32[]{:S(2)}) async-start(s8[8388608]{0:T(1024)(128)(4,1)} %bitcast.225), calls=%async_computation.41 | async-start | bytes 8388608
  390.0 9.4 %slice-start.38 = ((s8[8388608]{0:T(1024)(128)(4,1)}), s8[4194304]{0:T(1024)(128)(4,1)S(1)}, s32[]{:S(2)}) async-start(s8[8388608]{0:T(1024)(128)(4,1)} %bitcast.222), calls=%async_computation.39 | async-start | bytes 8388608
  394.8 9.4 %slice-start = ((s8[8388608]{0:T(1024)(128)(4,1)}), s8[4194304]{0:T(1024)(128)(4,1)S(1)}, s32[]{:S(2)}) async-start(s8[8388608]{0:T(1024)(128)(4,1)} %bitcast.164), calls=%async_computation.1 | async-start | bytes 8388608
  399.4 13.8 %slice-start.22 = ((s8[8388608]{0:T(1024)(128)(4,1)}), s8[4194304]{0:T(1024)(128)(4,1)S(1)}, s32[]{:S(2)}) async-start(s8[8388608]{0:T(1024)(128)(4,1)} %bitcast.196), calls=%async_computation.23 | async-start | bytes 8388608
  404.2 9.0 %slice-start.23 = ((s8[8388608]{0:T(1024)(128)(4,1)}), s8[4194304]{0:T(1024)(128)(4,1)S(1)}, s32[]{:S(2)}) async-start(s8[8388608]{0:T(1024)(128)(4,1)} %bitcast.196), calls=%async_computation.24 | async-start | bytes 8388608
  408.6 9.2 %slice-start.20 = ((s8[8388608]{0:T(1024)(128)(4,1)}), s8[4194304]{0:T(1024)(128)(4,1)S(1)}, s32[]{:S(2)}) async-start(s8[8388608]{0:T(1024)(128)(4,1)} %bitcast.193), calls=%async_computation.21 | async-start | bytes 8388608
  413.2 9.2 %slice-start.18 = ((s8[8388608]{0:T(1024)(128)(4,1)}), s8[4194304]{0:T(1024)(128)(4,1)S(1)}, s32[]{:S(2)}) async-start(s8[8388608]{0:T(1024)(128)(4,1)} %bitcast.190), calls=%async_computation.19 | async-start | bytes 8388608
  417.8 9.2 %slice-start.16 = ((s8[8388608]{0:T(1024)(128)(4,1)}), s8[4194304]{0:T(1024)(128)(4,1)S(1)}, s32[]{:S(2)}) async-start(s8[8388608]{0:T(1024)(128)(4,1)} %bitcast.187), calls=%async_computation.17 | async-start | bytes 8388608
  422.4 9.2 %slice-start.14 = ((s8[8388608]{0:T(1024)(128)(4,1)}), s8[4194304]{0:T(1024)(128)(4,1)S(1)}, s32[]{:S(2)}) async-start(s8[8388608]{0:T(1024)(128)(4,1)} %bitcast.184), calls=%async_computation.15 | async-start | bytes 8388608
  427.0 9.2 %slice-start.10 = ((s8[8388608]{0:T(1024)(128)(4,1)}), s8[4194304]{0:T(1024)(128)(4,1)S(1)}, s32[]{:S(2)}) async-start(s8[8388608]{0:T(1024)(128)(4,1)} %bitcast.178), calls=%async_computation.11 | async-start | bytes 8388608
  431.6 9.2 %slice-start.8 = ((s8[8388608]{0:T(1024)(128)(4,1)}), s8[4194304]{0:T(1024)(128)(4,1)S(1)}, s32[]{:S(2)}) async-start(s8[8388608]{0:T(1024)(128)(4,1)} %bitcast.175), calls=%async_computation.9 | async-start | bytes 8388608
  436.2 9.2 %slice-start.6 = ((s8[8388608]{0:T(1024)(128)(4,1)}), s8[4194304]{0:T(1024)(128)(4,1)S(1)}, s32[]{:S(2)}) async-start(s8[8388608]{0:T(1024)(128)(4,1)} %bitcast.172), calls=%async_computation.7 | async-start | bytes 8388608
  440.8 9.3 %slice-start.4 = ((s8[8388608]{0:T(1024)(128)(4,1)}), s8[4194304]{0:T(1024)(128)(4,1)S(1)}, s32[]{:S(2)}) async-start(s8[8388608]{0:T(1024)(128)(4,1)} %bitcast.169), calls=%async_computation.5 | async-start | bytes 8388608
  445.4 9.4 %slice-start.2 = ((s8[8388608]{0:T(1024)(128)(4,1)}), s8[4194304]{0:T(1024)(128)(4,1)S(1)}, s32[]{:S(2)}) async-start(s8[8388608]{0:T(1024)(128)(4,1)} %bitcast.166), calls=%async_computation.3 | async-start | bytes 8388608
  450.2 9.2 %slice-start.12 = ((s8[8388608]{0:T(1024)(128)(4,1)}), s8[4194304]{0:T(1024)(128)(4,1)S(1)}, s32[]{:S(2)}) async-start(s8[8388608]{0:T(1024)(128)(4,1)} %bitcast.181), calls=%async_computation.13 | async-start | bytes 8388608
  454.8 9.2 %slice-start.36 = ((s8[8388608]{0:T(1024)(128)(4,1)}), s8[4194304]{0:T(1024)(128)(4,1)S(1)}, s32[]{:S(2)}) async-start(s8[8388608]{0:T(1024)(128)(4,1)} %bitcast.217), calls=%async_computation.37 | async-start | bytes 8388608
  464.0 28.8 %slice-start.44 = ((s8[8388608]{0:T(1024)(128)(4,1)}), s8[4194304]{0:T(1024)(128)(4,1)S(1)}, s32[]{:S(2)}) async-start(s8[8388608]{0:T(1024)(128)(4,1)} %bitcast.232), calls=%async_computation.45 | async-start | bytes 8388608
  468.6 24.2 %slice-start.45 = ((s8[8388608]{0:T(1024)(128)(4,1)}), s8[4194304]{0:T(1024)(128)(4,1)S(1)}, s32[]{:S(2)}) async-start(s8[8388608]{0:T(1024)(128)(4,1)} %bitcast.232), calls=%async_computation.46 | async-start | bytes 8388608
  468.6 24.2 %copy-start.7 = (f32[64]{0:T(128)S(1)}, f32[64]{0:T(128)}, u32[]{:S(2)}) copy-start(f32[64]{0:T(128)} %convert_element_type.8) | copy-start | bytes 772
  (26 other events, 118.1 us)
Sparse Core Ops, SparseCore 0:
  8.9 60.9 all-gather.1
where the time goes:
time: 527 us; the launch traced here: 524 us
  local copies, waits for them, and re-layouts  169 us (32%)
  matrix products  163 us (31%)
  waiting for transfers between devices  147 us (28%)
  other arithmetic  26.5 us (5%)
  between operations  14 us (3%)
    dot_general x27, matrix products, convolve(): jnp.einsum('zpi,oi->zpo', window, tap_weight, preferred_element_type=jnp....  163 us
    slice x2, local copies, waits for them, and re-layouts, convolve(): framed[tap_z:tap_z + planes, tap_y:tap_y + rows, tap_x:tap_x + cols]  158 us
    ppermute x1, waiting for transfers between devices, extended(): lax.ppermute(tail, axis, [(i, (i + 1) % count) for i in range(ends)])  83.6 us
    all_gather x1, waiting for transfers between devices, body(): slab_planes = lax.all_gather(volume, 'filt', axis=0, tiled=True)  62.7 us
    concatenate x2, other arithmetic, extended(): jnp.concatenate([lax.ppermute(tail, axis, [(i, (i + 1) % count) for i in...  25.9 us
  transfers between devices with their start and end apart: 3, of which 2 were waited for; matrix products, arithmetic and copies ran while one was open for 1% of the time, Pallas kernels for 0%

commit v1 on v0

--- a/solution.py
+++ b/solution.py
@@ -45,7 +45,24 @@
 
 
 def body(volume, weights, bias):
-    slab_planes = lax.all_gather(volume, "filt", axis=0, tiled=True)
+    ways, here, step = (lax.axis_size("filt"), lax.axis_index("filt"), volume.shape[0])
+    shape = [n * ways if d == 0 else n for d, n in enumerate(volume.shape)]
+    slab_planes = lax.dynamic_update_slice_in_dim(
+        jnp.zeros(shape, volume.dtype), volume, here * step, axis=0
+    )
+    going_up = going_down = volume
+    for far in range(1, ways // 2 + 1):
+        going_up = lax.ppermute(going_up, "filt", [(d, (d + 1) % ways) for d in range(ways)])
+        slab_planes = lax.dynamic_update_slice_in_dim(
+            slab_planes, going_up, (here - far) % ways * step, axis=0
+        )
+        if 2 * far < ways:
+            going_down = lax.ppermute(
+                going_down, "filt", [(d, (d - 1) % ways) for d in range(ways)]
+            )
+            slab_planes = lax.dynamic_update_slice_in_dim(
+                slab_planes, going_down, (here + far) % ways * step, axis=0
+            )
     padded = extended(slab_planes, (("slab", 0),), 1)
     return convolve(padded, weights, bias)
 

time: 527 us -> 543 us (1.030); the launches traced: 524 us -> 535 us
  between operations: 14 us -> 0.95 us
  other arithmetic: 26.5 us -> 34.9 us
  starting transfers between devices: 4.93 us -> 11.1 us
  local copies, waits for them, and re-layouts: 169 us -> 175 us
    all_gather x1 -> x0, waiting for transfers between devices: 62.7 us -> none  [body(): slab_planes = lax.all_gather(volume, 'filt', axis=0, tiled=True)]
    ppermute x0 -> x3, waiting for transfers between devices: none -> 62.2 us  [the longest x2 62.2 us: body(): lax.ppermute(going_up, 'filt', [(d, (d + 1) % ways) for d in range(ways)])]
    concatenate x2, other arithmetic: 25.9 us -> 34.4 us  [extended(): jnp.concatenate([lax.ppermute(tail, axis, [(i, (i + 1) % count) for i in...]
    dynamic_update_slice x0 -> x4, local copies, waits for them, and re-layouts: none -> 5.84 us  [the longest x2 3.71 us: body(): lax.dynamic_update_slice_in_dim(slab_planes, going_up, (here - far) % way...]
  transfers between devices with their start and end apart: 3 -> 5, of which waited for: 2 -> 3; matrix products, arithmetic and copies ran while one was open for 1% -> 1% of each run, Pallas kernels for 0% -> 0%
where the time goes in v1:
time: 543 us; the launch traced here: 535 us
  local copies, waits for them, and re-layouts  175 us (32%)
  matrix products  162 us (30%)
  waiting for transfers between devices  150 us (28%)
  other arithmetic  34.9 us (6%)
  starting transfers between devices  11.1 us (2%)
    slice x2, local copies, waits for them, and re-layouts, convolve(): framed[tap_z:tap_z + planes, tap_y:tap_y + rows, tap_x:tap_x + cols]  162 us
    dot_general x27, matrix products, convolve(): jnp.einsum('zpi,oi->zpo', window, tap_weight, preferred_element_type=jnp....  162 us
    ppermute x1, waiting for transfers between devices, extended(): lax.ppermute(tail, axis, [(i, (i + 1) % count) for i in range(ends)])  88.2 us
    ppermute x2, waiting for transfers between devices, body(): lax.ppermute(going_up, 'filt', [(d, (d + 1) % ways) for d in range(ways)])  62.2 us
    concatenate x2, other arithmetic, extended(): jnp.concatenate([lax.ppermute(tail, axis, [(i, (i + 1) % count) for i in...  34.4 us
  transfers between devices with their start and end apart: 5, of which 3 were waited for; matrix products, arithmetic and copies ran while one was open for 1% of the time, Pallas kernels for 0%

profile of v1, /device:TPU:0, one launch (start us, length us, event | category | flops | bytes accessed | tf_op | source)
XLA Modules:
  0.0 534.8 jit_solution(12732265327044835706)
XLA Ops:
  2.5 43.9 %collective-permute-done = bf16[1,64,64,256]{3,2,1,0:T(8,128)(2,1)} collective-permute-done((bf16[1,64,64,256]{3,2,1,0:T(8,128)(2,1)}, bf16[1,64,64,256]{3,2,1,0:T(8,128)(2,1)}, u32[]{:S(2)}, u32[]{:S(2)}) %collective-permute-start) | collective-permute-done | bytes 2097184 | tf_op jit(solution)/shard_map/ppermute | solution.py:55
  53.9 18.3 %collective-permute-done.2 = bf16[1,64,64,256]{3,2,1,0:T(8,128)(2,1)} collective-permute-done((bf16[1,64,64,256]{3,2,1,0:T(8,128)(2,1)}, bf16[1,64,64,256]{3,2,1,0:T(8,128)(2,1)}, u32[]{:S(2)}, u32[]{:S(2)}) %collective-permute-start.2) | collective-permute-done | bytes 2097184 | tf_op jit(solution)/shard_map/ppermute | solution.py:55
  74.4 5.0 collective-permute-start.3
  81.2 88.2 %collective-permute-done.3 = bf16[1,64,64,256]{3,2,1,0:T(8,128)(2,1)S(1)} collective-permute-done((bf16[1,64,64,256]{3,2,1,0:T(8,128)(2,1)S(1)}, bf16[1,64,64,256]{3,2,1,0:T(8,128)(2,1)S(1)}, u32[]{:S(2)}, u32[]{:S(2)}) %collective-permute-start.3) | collective-permute-done | bytes 2097184 | tf_op jit(solution)/shard_map/ppermute | solution.py:15
  172.1 21.5 %select_maximum_fusion = bf16[6,66,66,256]{3,2,1,0:T(8,128)(2,1)} fusion(bf16[1,64,64,256]{3,2,1,0:T(8,128)(2,1)S(1)} %collective-permute-done.4, bf16[4,64,64,256]{3,2,1,0:T(8,128)(2,1)S(1)} %constant_dynamic-update-slice_fusion, bf16[1,64,64,256]{3,2,1,0:T(8,128)(2,1)S(1)} %collective-permute-done.3), kind=kLoop, calls=%fused_computation.7 | loop fusion | flops 127125504 | bytes 25964544 | tf_op jit(solution)/shard_map/concatenate | solution.py:13
  193.6 126.6 %fusion.111 = (bf16[4,64,64,256]{3,2,1,0:T(8,128)(2,1)}, bf16[4,64,64,256]{3,2,1,0:T(8,128)(2,1)}, bf16[4,64,64,256]{3,2,1,0:T(8,128)(2,1)}, bf16[4,64,64,256]{3...) fusion(bf16[6,66,66,256]{3,2,1,0:T(8,128)(2,1)} %select_maximum, ...), kind=kLoop, calls=%fused_computation.126 | loop fusion | bytes 318767104 | tf_op jit(solution)/shard_map/slice | solution.py:35
  320.2 35.6 %fusion.112 = (bf16[4,64,64,256]{3,2,1,0:T(8,128)(2,1)}, bf16[4,64,64,256]{3,2,1,0:T(8,128)(2,1)}, bf16[4,64,64,256]{3,2,1,0:T(8,128)(2,1)}, bf16[4,64,64,256]{3,2,1,0:T(8,128)(2,1)}, bf16[4,64,64,256]{3,2,1,0:T(8,128)(2,1)}) fusion(bf16[6,66,66,256]{3,2,1,0:T(8,128)(2,1)} %select_maximum_fusion), kind=kLoop, calls=%fused_computation.127 | loop fusion | bytes 83886080 | tf_op jit(solution)/shard_map/slice | solution.py:35
  355.8 6.2 %fusion.59 = f32[4,4096,64]{1,2,0:T(8,128)S(1)} fusion(bf16[4,4096,256]{2,1,0:T(8,128)(2,1)} %bitcast.233, bf16[64,27,256]{2,0,1:T(8,128)(2,1)} %param.4), kind=kOutput, calls=%fused_computation.70 | convolution fusion | flops 536870912 | bytes 12615680 | tf_op jit(solution)/shard_map/zpi,oi->zpo/dot_general | solution.py:39
  362.0 5.6 %fusion.61 = f32[4,4096,64]{1,2,0:T(8,128)} fusion(bf16[4,4096,256]{2,1,0:T(8,128)(2,1)S(1)} %bitcast.229, bf16[64,27,256]{2,0,1:T(8,128)(2,1)} %param.4), kind=kOutput, calls=%fused_computation.72 | convolution fusion | flops 536870912 | bytes 12615680 | tf_op jit(solution)/shard_map/zpi,oi->zpo/dot_general | solution.py:39
  367.7 5.6 %fusion.63 = f32[4,4096,64]{1,2,0:T(8,128)} fusion(bf16[4,4096,256]{2,1,0:T(8,128)(2,1)S(1)} %bitcast.225, bf16[64,27,256]{2,0,1:T(8,128)(2,1)} %param.4), kind=kOutput, calls=%fused_computation.74 | convolution fusion | flops 536870912 | bytes 12615680 | tf_op jit(solution)/shard_map/zpi,oi->zpo/dot_general | solution.py:39
  373.3 5.5 %fusion.65 = f32[4,4096,64]{1,2,0:T(8,128)} fusion(bf16[4,4096,256]{2,1,0:T(8,128)(2,1)S(1)} %bitcast.219, bf16[64,27,256]{2,0,1:T(8,128)(2,1)} %param.4), kind=kOutput, calls=%fused_computation.76 | convolution fusion | flops 536870912 | bytes 12615680 | tf_op jit(solution)/shard_map/zpi,oi->zpo/dot_general | solution.py:39
  378.7 5.5 %fusion.67 = f32[4,4096,64]{1,2,0:T(8,128)} fusion(bf16[4,4096,256]{2,1,0:T(8,128)(2,1)S(1)} %bitcast.213, bf16[64,27,256]{2,0,1:T(8,128)(2,1)} %param.4), kind=kOutput, calls=%fused_computation.78 | convolution fusion | flops 536870912 | bytes 12615680 | tf_op jit(solution)/shard_map/zpi,oi->zpo/dot_general | solution.py:39
  384.3 5.5 %fusion.69 = f32[4,4096,64]{1,2,0:T(8,128)} fusion(bf16[4,4096,256]{2,1,0:T(8,128)(2,1)S(1)} %bitcast.210, bf16[64,27,256]{2,0,1:T(8,128)(2,1)} %param.4), kind=kOutput, calls=%fused_computation.80 | convolution fusion | flops 536870912 | bytes 12615680 | tf_op jit(solution)/shard_map/zpi,oi->zpo/dot_general | solution.py:39
  389.9 4.8 fusion.71
  394.7 12.9 %pad_maximum_fusion.1 = (bf16[4,64,64,256]{3,2,1,0:T(8,128)(2,1)S(1)}, bf16[4,64,64,256]{3,2,1,0:T(8,128)(2,1)}) fusion(bf16[4,64,64,256]{3,2,1,0:T(8,128)(2,1)S(1)} %bitcast.165, bf16[1,64,64,256]{3,2,1,0:T(8,128)(2,1)S(1)} %copy-done.3, bf16[1,64,64,256]{3,2,1,0:T(8,128)(2,1)S(1)} %copy-done.5), kind=kLoop, calls=%fused_computation.14 | loop fusion | flops 8388608 | bytes 29360128 | tf_op jit(solution)/shard_map/concatenate | solution.py:13
  407.6 4.6 fusion.75
  412.2 4.6 fusion.73
  416.8 4.6 fusion.77
  421.4 4.6 fusion.79
  426.1 4.6 fusion.81
  430.7 4.6 fusion.34
  439.9 4.6 fusion.38
  444.5 4.8 fusion.42
  449.2 4.7 fusion.44
  458.5 4.6 fusion.48
  463.1 4.7 fusion.50
  467.8 4.6 fusion.52
  477.0 4.6 fusion.56
  481.6 4.7 fusion.40
  486.2 4.9 fusion.32
  491.1 18.2 %fusion.23 = f32[4,4096,64]{1,2,0:T(8,128)} fusion(f32[4,4096,64]{1,2,0:T(8,128)S(1)} %fusion.59, f32[4,4096,64]{1,2,0:T(8,128)} %fusion.61, f32[4,4096,64]{1,2,0:T(8,128)} %fusion.63, f32[4,4096,64]{1,2,0:T(8,128)} %fusion.65, f32[4,4096,64]{1,2,0:T(8,128)} %fusion.67, f32[4,4096,64]{1,2,0:T(8,128)} %fusion.69, f32[4,4096,64]{1,2,0:T(8,128)} %fusion.71, ...), kind=kOutput, calls=%fused_computation.34 | convolution fusion | flops 549453824 | bytes 62947328 | tf_op jit(solution)/shard_map/zpi,oi->zpo/dot_general | solution.py:39
  509.3 22.0 %fusion.31 = bf16[4,4096,64]{1,2,0:T(8,128)(2,1)S(1)} fusion(f32[4,4096,64]{1,2,0:T(8,128)} %fusion.32, f32[4,4096,64]{1,2,0:T(8,128)} %fusion.34, f32[4,4096,64]{1,2,0:T(8,128)} %fusion.36, f32[4,4096,64]{1,2,0:T(8,128)} %fusion.38, f32[4,4096,64]{1,2,0:T(8,128)} %fusion.40, f32[4,4096,64]{1,2,0:T(8,128)} %fusion.42, f32[4,4096,64]{1,2,0:T(8,128)} %fusion.44, ...), kind=kOutput, calls=%fused_computation.42 | convolution fusion | flops 556793856 | bytes 69239040 | tf_op jit(solution)/shard_map/zpi,oi->zpo/dot_general | solution.py:39
  (157 shorter events, 33.6 us)
Async XLA Ops:
  0.0 49.8 %copy-start.6 = (bf16[1,64,64,256]{3,2,1,0:T(8,128)(2,1)S(1)}, bf16[1,64,64,256]{3,2,1,0:T(8,128)(2,1)}, u32[]{:S(2)}) copy-start(bf16[1,64,64,256]{3,2,1,0:T(8,128)(2,1)} %param.3) | copy-start | bytes 6291460
  0.0 46.4 %collective-permute-start = (bf16[1,64,64,256]{3,2,1,0:T(8,128)(2,1)}, bf16[1,64,64,256]{3,2,1,0:T(8,128)(2,1)}, u32[]{:S(2)}, u32[]{:S(2)}) collective-permute-start(bf16[1,64,64,256]{3,2,1,0:T(8,128)(2,1)} %param.3), channel_id=1, source_target_pairs={{0,1},{1,2},{2,3},{3,0},{4,5},{5,6},{6,7},{7,4},{8,9},{9,10},{10,1... | collective-permute-start | bytes 6291464 | tf_op jit(solution)/shard_map/ppermute | solution.py:55
  0.5 51.6 %collective-permute-start.1 = (bf16[1,64,64,256]{3,2,1,0:T(8,128)(2,1)}, bf16[1,64,64,256]{3,2,1,0:T(8,128)(2,1)}, u32[]{:S(2)}, u32[]{:S(2)}) collective-permute-start(bf16[1,64,64,256]{3,2,1,0:T(8,128)(2,1)} %param.3), channel_id=1, source_target_pairs={{0,3},{1,0},{2,1},{3,2},{4,7},{5,4},{6,5},{7,6},{8,11},{9,8},{10,9... | collective-permute-start | bytes 6291464 | tf_op jit(solution)/shard_map/ppermute | solution.py:60
  46.4 25.8 %collective-permute-start.2 = (bf16[1,64,64,256]{3,2,1,0:T(8,128)(2,1)}, bf16[1,64,64,256]{3,2,1,0:T(8,128)(2,1)}, u32[]{:S(2)}, u32[]{:S(2)}) collective-permute-start(bf16[1,64,64,256]{3,2,1,0:T(8,128)(2,1)} %collective-permute-done), channel_id=1, source_target_pairs={{0,1},{1,2},{2,3},{3,0},{4,5},{5,6},{6,7},{7,4},{8,9},{9,10},{10,1... | collective-permute-start | bytes 6291464 | tf_op jit(solution)/shard_map/ppermute | solution.py:55
  52.0 28.6 %copy-start.9 = (bf16[64]{0:T(256)(128)(2,1)S(1)}, bf16[64]{0:T(256)(128)(2,1)}, u32[]{:S(2)}) copy-start(bf16[64]{0:T(256)(128)(2,1)} %param.5) | copy-start | bytes 388
  74.0 95.4 %copy-start = (bf16[4,64,64,256]{3,2,1,0:T(8,128)(2,1)}, bf16[4,64,64,256]{3,2,1,0:T(8,128)(2,1)S(1)}, u32[]{:S(2)}) copy-start(bf16[4,64,64,256]{3,2,1,0:T(8,128)(2,1)S(1)} %constant_dynamic-update-slice_fusion) | copy-start | bytes 25165828
  74.4 95.1 %collective-permute-start.3 = (bf16[1,64,64,256]{3,2,1,0:T(8,128)(2,1)S(1)}, bf16[1,64,64,256]{3,2,1,0:T(8,128)(2,1)S(1)}, u32[]{:S(2)}, u32[]{:S(2)}) collective-permute-start(bf16[1,64,64,256]{3,2,1,0:T(8,128)(2,1)S(1)} %get-tuple-element.31), channel_id=1, source_target_pairs={{0,4},{4,8},{8,12},{12,16},{16,20},{20,24},{24,28},{1,5},{5,9},{9,... | collective-permute-start | bytes 6291464 | tf_op jit(solution)/shard_map/ppermute | solution.py:15
  79.3 90.1 %collective-permute-start.4 = (bf16[1,64,64,256]{3,2,1,0:T(8,128)(2,1)S(1)}, bf16[1,64,64,256]{3,2,1,0:T(8,128)(2,1)S(1)}, u32[]{:S(2)}, u32[]{:S(2)}) collective-permute-start(bf16[1,64,64,256]{3,2,1,0:T(8,128)(2,1)S(1)} %get-tuple-element.32), channel_id=1, source_target_pairs={{4,0},{8,4},{12,8},{16,12},{20,16},{24,20},{28,24},{5,1},{9,5},{13... | collective-permute-start | bytes 6291464 | tf_op jit(solution)/shard_map/ppermute | solution.py:17
  355.8 11.8 %slice-start.40 = ((s8[8388608]{0:T(1024)(128)(4,1)}), s8[4194304]{0:T(1024)(128)(4,1)S(1)}, s32[]{:S(2)}) async-start(s8[8388608]{0:T(1024)(128)(4,1)} %bitcast.223), calls=%async_computation.40 | async-start | bytes 8388608
  362.0 11.3 %slice-start.36 = ((s8[8388608]{0:T(1024)(128)(4,1)}), s8[4194304]{0:T(1024)(128)(4,1)S(1)}, s32[]{:S(2)}) async-start(s8[8388608]{0:T(1024)(128)(4,1)} %bitcast.217), calls=%async_computation.36 | async-start | bytes 8388608
  367.6 11.1 %slice-start.32 = ((s8[8388608]{0:T(1024)(128)(4,1)}), s8[4194304]{0:T(1024)(128)(4,1)S(1)}, s32[]{:S(2)}) async-start(s8[8388608]{0:T(1024)(128)(4,1)} %bitcast.211), calls=%async_computation.32 | async-start | bytes 8388608
  373.2 11.0 %slice-start.30 = ((s8[8388608]{0:T(1024)(128)(4,1)}), s8[4194304]{0:T(1024)(128)(4,1)S(1)}, s32[]{:S(2)}) async-start(s8[8388608]{0:T(1024)(128)(4,1)} %bitcast.208), calls=%async_computation.30 | async-start | bytes 8388608
  378.7 11.1 %slice-start.28 = ((s8[8388608]{0:T(1024)(128)(4,1)}), s8[4194304]{0:T(1024)(128)(4,1)S(1)}, s32[]{:S(2)}) async-start(s8[8388608]{0:T(1024)(128)(4,1)} %bitcast.205), calls=%async_computation.28 | async-start | bytes 8388608
  384.3 10.4 %slice-start = ((s8[8388608]{0:T(1024)(128)(4,1)}), s8[4194304]{0:T(1024)(128)(4,1)S(1)}, s32[]{:S(2)}) async-start(s8[8388608]{0:T(1024)(128)(4,1)} %bitcast.164), calls=%async_computation | async-start | bytes 8388608
  389.9 22.3 %slice-start.44 = ((s8[8388608]{0:T(1024)(128)(4,1)}), s8[4194304]{0:T(1024)(128)(4,1)S(1)}, s32[]{:S(2)}) async-start(s8[8388608]{0:T(1024)(128)(4,1)} %bitcast.230), calls=%async_computation.44 | async-start | bytes 8388608
  394.7 17.5 %slice-start.45 = ((s8[8388608]{0:T(1024)(128)(4,1)}), s8[4194304]{0:T(1024)(128)(4,1)S(1)}, s32[]{:S(2)}) async-start(s8[8388608]{0:T(1024)(128)(4,1)} %bitcast.230), calls=%async_computation.45 | async-start | bytes 8388608
  407.6 9.2 %slice-start.42 = ((s8[8388608]{0:T(1024)(128)(4,1)}), s8[4194304]{0:T(1024)(128)(4,1)S(1)}, s32[]{:S(2)}) async-start(s8[8388608]{0:T(1024)(128)(4,1)} %bitcast.226), calls=%async_computation.42 | async-start | bytes 8388608
  412.2 9.2 %slice-start.38 = ((s8[8388608]{0:T(1024)(128)(4,1)}), s8[4194304]{0:T(1024)(128)(4,1)S(1)}, s32[]{:S(2)}) async-start(s8[8388608]{0:T(1024)(128)(4,1)} %bitcast.220), calls=%async_computation.38 | async-start | bytes 8388608
  416.8 9.2 %slice-start.34 = ((s8[8388608]{0:T(1024)(128)(4,1)}), s8[4194304]{0:T(1024)(128)(4,1)S(1)}, s32[]{:S(2)}) async-start(s8[8388608]{0:T(1024)(128)(4,1)} %bitcast.214), calls=%async_computation.34 | async-start | bytes 8388608
  421.4 9.2 %slice-start.24 = ((s8[8388608]{0:T(1024)(128)(4,1)}), s8[4194304]{0:T(1024)(128)(4,1)S(1)}, s32[]{:S(2)}) async-start(s8[8388608]{0:T(1024)(128)(4,1)} %bitcast.199), calls=%async_computation.24 | async-start | bytes 8388608
  426.1 9.2 %slice-start.22 = ((s8[8388608]{0:T(1024)(128)(4,1)}), s8[4194304]{0:T(1024)(128)(4,1)S(1)}, s32[]{:S(2)}) async-start(s8[8388608]{0:T(1024)(128)(4,1)} %bitcast.196), calls=%async_computation.22 | async-start | bytes 8388608
  430.7 9.2 %slice-start.20 = ((s8[8388608]{0:T(1024)(128)(4,1)}), s8[4194304]{0:T(1024)(128)(4,1)S(1)}, s32[]{:S(2)}) async-start(s8[8388608]{0:T(1024)(128)(4,1)} %bitcast.193), calls=%async_computation.20 | async-start | bytes 8388608
  435.3 9.2 %slice-start.18 = ((s8[8388608]{0:T(1024)(128)(4,1)}), s8[4194304]{0:T(1024)(128)(4,1)S(1)}, s32[]{:S(2)}) async-start(s8[8388608]{0:T(1024)(128)(4,1)} %bitcast.190), calls=%async_computation.18 | async-start | bytes 8388608
  439.9 9.4 %slice-start.16 = ((s8[8388608]{0:T(1024)(128)(4,1)}), s8[4194304]{0:T(1024)(128)(4,1)S(1)}, s32[]{:S(2)}) async-start(s8[8388608]{0:T(1024)(128)(4,1)} %bitcast.187), calls=%async_computation.16 | async-start | bytes 8388608
  444.5 9.5 %slice-start.14 = ((s8[8388608]{0:T(1024)(128)(4,1)}), s8[4194304]{0:T(1024)(128)(4,1)S(1)}, s32[]{:S(2)}) async-start(s8[8388608]{0:T(1024)(128)(4,1)} %bitcast.184), calls=%async_computation.14 | async-start | bytes 8388608
  449.2 9.3 %slice-start.12 = ((s8[8388608]{0:T(1024)(128)(4,1)}), s8[4194304]{0:T(1024)(128)(4,1)S(1)}, s32[]{:S(2)}) async-start(s8[8388608]{0:T(1024)(128)(4,1)} %bitcast.181), calls=%async_computation.12 | async-start | bytes 8388608
  458.5 9.3 %slice-start.6 = ((s8[8388608]{0:T(1024)(128)(4,1)}), s8[4194304]{0:T(1024)(128)(4,1)S(1)}, s32[]{:S(2)}) async-start(s8[8388608]{0:T(1024)(128)(4,1)} %bitcast.172), calls=%async_computation.6 | async-start | bytes 8388608
  463.1 9.3 %slice-start.4 = ((s8[8388608]{0:T(1024)(128)(4,1)}), s8[4194304]{0:T(1024)(128)(4,1)S(1)}, s32[]{:S(2)}) async-start(s8[8388608]{0:T(1024)(128)(4,1)} %bitcast.169), calls=%async_computation.4 | async-start | bytes 8388608
  472.4 9.2 %slice-start.26 = ((s8[8388608]{0:T(1024)(128)(4,1)}), s8[4194304]{0:T(1024)(128)(4,1)S(1)}, s32[]{:S(2)}) async-start(s8[8388608]{0:T(1024)(128)(4,1)} %bitcast.202), calls=%async_computation.26 | async-start | bytes 8388608
  476.9 9.3 %slice-start.8 = ((s8[8388608]{0:T(1024)(128)(4,1)}), s8[4194304]{0:T(1024)(128)(4,1)S(1)}, s32[]{:S(2)}) async-start(s8[8388608]{0:T(1024)(128)(4,1)} %bitcast.175), calls=%async_computation.8 | async-start | bytes 8388608
  481.5 9.6 %slice-start.46 = ((s8[8388608]{0:T(1024)(128)(4,1)}), s8[4194304]{0:T(1024)(128)(4,1)S(1)}, s32[]{:S(2)}) async-start(s8[8388608]{0:T(1024)(128)(4,1)} %bitcast.235), calls=%async_computation.46 | async-start | bytes 8388608
  491.1 18.2 %copy-start.8 = (f32[64]{0:T(128)S(1)}, f32[64]{0:T(128)}, u32[]{:S(2)}) copy-start(f32[64]{0:T(128)} %convert_element_type.8) | copy-start | bytes 772
  (31 other events, 153.9 us)
